TPU v7x, 32 devices: a whole 2x2x4 slice. The times are simulated.
32 devices in a mesh: run: 8 (over y, x, core), seg: 4 (over z).
Axes of the slice: x: 2, y: 2, z: 4, core: 2. Of those that a mesh axis runs over, the one named last changes fastest.
Arguments:
- diag_blocks: float32 [4, 16, 256, 256], P('seg', 'run'), as said below
- coupling: float32 [4, 16, 256, 256], P('seg', 'run')
- rhs: float32 [4, 16, 256, 128], P('seg', 'run'), may hold values from -0.65 to 0.65
Outputs:
- solution: float32 [4, 16, 256, 128], P('seg', 'run')
Inputs may be any that keep to these rules, and one draw needn't show every extreme that they name: Together with coupling, diag_blocks makes A symmetric positive definite.
All inputs are finite; a program needn't handle non-finite values.
Results may differ from a plain program's by a relative error of at most 0.0003.
Values sent between devices are 32-bit elements; how exact they have to be, the bound alone decides.
A program may use at most 128 MiB of HBM per device.

v0:
```python
import functools

import jax
import jax.numpy as jnp
from jax import lax
from jax.experimental import pallas as pl
from jax.experimental.pallas import tpu as pltpu
from jax.sharding import PartitionSpec as P

MESH = pl.DeviceIdType.MESH
HIGH = lax.Precision.HIGHEST
ROWS = 8
LANES = 128


def dot(a, b):
    return jnp.dot(a, b, precision=HIGH, preferred_element_type=jnp.float32)


def dot_nt(a, b):
    return lax.dot_general(
        a, b, (((1,), (1,)), ((), ())), precision=HIGH, preferred_element_type=jnp.float32
    )


def spd_inverse_tile(rows):
    count = len(rows)
    width = rows[0].shape[1]
    shape = (ROWS, width)
    sub = lax.broadcasted_iota(jnp.int32, shape, 0)
    lane = lax.broadcasted_iota(jnp.int32, shape, 1)
    rows = list(rows)
    for k in range(count):
        first = k * ROWS
        panel = rows[k]
        cols = [jnp.broadcast_to(panel[:, first + j : first + j + 1], shape) for j in range(ROWS)]
        for j in range(ROWS):
            here = sub == j
            pivot = jnp.broadcast_to(cols[j][j : j + 1, :], shape)
            inverse = 1.0 / pivot
            factor = jnp.where(here, -1.0, cols[j])
            panel = jnp.where(lane == first + j, jnp.where(here, 1.0, 0.0), panel)
            line = jnp.broadcast_to(panel[j : j + 1, :], shape)
            panel = jnp.where(here, 0.0, panel) - (factor * line) * inverse
            for m in range(j + 1, ROWS):
                line = jnp.broadcast_to(cols[m][j : j + 1, :], shape)
                cols[m] = jnp.where(here, 0.0, cols[m]) - (factor * line) * inverse
        lines = [jnp.broadcast_to(panel[j : j + 1, :], shape) for j in range(ROWS)]
        inside = jnp.logical_and(lane >= first, lane < first + ROWS)
        for i in range(count):
            if i == k:
                continue
            old = rows[i]
            terms = [
                jnp.broadcast_to(old[:, first + j : first + j + 1], shape) * lines[j]
                for j in range(ROWS)
            ]
            while len(terms) > 1:
                terms = [terms[t] + terms[t + 1] for t in range(0, len(terms), 2)]
            rows[i] = jnp.where(inside, 0.0, old) - terms[0]
        rows[k] = panel
    return rows


def invert(node, x, tile, work, late):
    half = tile.shape[0]
    top, low = slice(0, half), slice(half, 2 * half)
    tile[...] = node[0]

    @pl.loop(0, 2)
    def _(step):
        rows = spd_inverse_tile([tile[i : i + ROWS, :] for i in range(0, half, ROWS)])
        for i, row in enumerate(rows):
            tile[i * ROWS : (i + 1) * ROWS, :] = row

        @pl.when(step == 0)
        def _():
            late()
            x[top, top] = tile[...]
            work[0] = dot(tile[...], node[1])
            work[1] = work[0].T
            tile[...] = node[2] - dot(work[1], node[1])

        @pl.when(step == 1)
        def _():
            corner = -dot(tile[...], work[1])
            x[low, low] = tile[...]
            x[low, top] = corner
            x[top, low] = -dot(work[0], tile[...])
            x[top, top] = x[top, top] - dot(work[0], corner)


def kernel(
    runs,
    total,
    diag,
    coup,
    rhs,
    out,
    x,
    tile,
    work,
    node,
    source,
    e_turned,
    w_p,
    w_q,
    keep_p,
    keep_q,
    keep_y,
    send_d,
    send_m,
    send_b,
    first_d,
    first_b,
    got_d,
    got_b,
    got_link,
    got_x,
    before,
    value,
    sent,
    sent_first,
    sent_value,
    come_d,
    come_b,
    come_m,
    come_x,
):
    slabs, order = diag.shape[:2]
    inner = slabs - 1
    half = order // 2
    top, low = slice(0, half), slice(half, order)
    me = lax.axis_index("seg") * runs + lax.axis_index("run")
    depth = total.bit_length() - 1
    strides = [1 << i for i in range(depth)]
    root = me == total - 1
    inside = jnp.logical_not(root)
    even = lax.rem(me, 2) == 0
    odd = jnp.logical_not(even)
    parents = [lax.rem(me + 1, 2 * s) == 0 for s in strides]
    level = sum(jnp.where(parent, 1, 0) for parent in parents)
    span = 1 + sum(jnp.where(parent, s, 0) for s, parent in zip(strides, parents))
    next_above = lax.rem(me + span, 4 * span) == 2 * span - 1
    up = jnp.where(next_above, 1, 0)
    peer_p = jnp.where(next_above, me + span, me - span)
    peer_q = jnp.where(next_above, me - span, me + span)
    has_q = jnp.logical_and(inside, jnp.logical_and(peer_q >= 0, peer_q < total))
    slot_p = 1 + 2 * level + (1 - up)
    slot_q = 1 + 2 * level + up

    def copy(source_ref, target_ref, send_sem, recv_sem, peer):
        return pltpu.make_async_remote_copy(
            src_ref=source_ref,
            dst_ref=target_ref,
            send_sem=send_sem,
            recv_sem=recv_sem,
            device_id=(lax.rem(peer, runs), lax.div(peer, runs)),
            device_id_type=MESH,
        )

    barrier = pltpu.get_barrier_semaphore()
    met = [lax.rem(me + 1, s) == 0 for s in strides]
    peers = sum(
        jnp.where(jnp.logical_and(here, ok), 1, 0)
        for s, here in zip(strides, met)
        for ok in (me >= s, me + s < total)
    )
    for s, here in zip(strides, met):
        for ok, peer in ((me >= s, me - s), (me + s < total, me + s)):

            @pl.when(jnp.logical_and(here, ok))
            def _():
                pl.semaphore_signal(
                    barrier,
                    inc=1,
                    device_id=(lax.rem(peer, runs), lax.div(peer, runs)),
                    device_id_type=MESH,
                )

    def first_head(peer):
        return copy(first_d.at[0], got_d.at[0, 0], sent_first.at[0], come_d.at[0], peer)

    def first_tail(peer):
        return copy(
            first_d.at[pl.ds(1, 2)], got_d.at[0, pl.ds(1, 2)], sent_first.at[1], come_d.at[1], peer
        )

    def first_link(peer):
        return copy(send_m, got_link.at[1], sent_first.at[2], come_m.at[1], peer)

    def first_thin(peer):
        return copy(first_b, got_b.at[0], sent_first.at[3], come_b.at[0], peer)

    def head(role, slot, peer):
        return copy(
            send_d.at[role, 0], got_d.at[slot, 0], sent.at[role], come_d.at[2 * slot], peer
        )

    def tail(role, slot, peer):
        return copy(
            send_d.at[role, pl.ds(1, 2)],
            got_d.at[slot, pl.ds(1, 2)],
            sent.at[2 + role],
            come_d.at[2 * slot + 1],
            peer,
        )

    def thin(role, slot, peer):
        return copy(send_b.at[role], got_b.at[slot], sent.at[4 + role], come_b.at[slot], peer)

    def coupled(side, peer):
        return copy(send_m, got_link.at[side], sent.at[6], come_m.at[side], peer)

    def each_source(act):
        @pl.when(inside)
        def _():
            act(0, me + 1)

        for i, s in enumerate(strides):
            for way, (ok, peer) in enumerate(((me >= s, me - s), (me + s < total, me + s))):

                @pl.when(jnp.logical_and(parents[i], ok))
                def _():
                    act(1 + 2 * i + way, peer)

    e_turned[...] = jnp.where(me == 0, jnp.zeros_like(coup[0]), coup[0]).T
    node[0] = diag[0, top, top]
    node[1] = diag[0, top, low]
    node[2] = diag[0, low, low]
    source[...] = rhs[0]
    for i in range(inner):
        final = i == inner - 1
        f_turned = coup.at[i + 1]
        invert(node, x, tile, work, lambda: None)
        w_p[...] = dot(e_turned[...], x[...])

        def put(block, rows, columns):
            term = dot_nt(w_p[rows, :], e_turned[columns, :])
            first_d[block] = -term if i == 0 else first_d[block] - term

        put(0, top, top)
        if final:
            pl.semaphore_wait(barrier, peers)

            @pl.when(me > 0)
            def _():
                first_head(me - 1).start()

        put(1, top, low)
        put(2, low, low)
        if final:

            @pl.when(me > 0)
            def _():
                first_tail(me - 1).start()

        w_q[...] = dot(f_turned[...], x[...])
        node[0] = diag[i + 1, top, top] - dot_nt(w_q[top, :], f_turned[top, :])
        node[1] = diag[i + 1, top, low] - dot_nt(w_q[top, :], f_turned[low, :])
        node[2] = diag[i + 1, low, low] - dot_nt(w_q[low, :], f_turned[low, :])
        if final:

            @pl.when(odd)
            def _():
                send_m[...] = -dot_nt(w_q[...], e_turned[...])
                first_link(me - 1).start()

            @pl.when(even)
            def _():
                got_link[0] = -dot_nt(w_p[...], f_turned[...])

        keep_y[i] = dot(x[...], source[...])
        term = dot(e_turned[...], keep_y[i])
        first_b[...] = -term if i == 0 else first_b[...] - term
        if final:

            @pl.when(me > 0)
            def _():
                first_thin(me - 1).start()

        source[...] = rhs[i + 1] - dot(f_turned[...], keep_y[i])
        keep_p[i] = dot_nt(x[...], e_turned[...])
        keep_q[i] = dot_nt(x[...], f_turned[...])
        if not final:
            e_turned[...] = -dot_nt(w_p[...], f_turned[...])

    def add_head(slot, peer):
        head(0, slot, peer).wait_recv()
        node[0] = node[0] + got_d[slot, 0]

    def add_tail(slot, peer):
        tail(0, slot, peer).wait_recv()
        node[1] = node[1] + got_d[slot, 1]
        node[2] = node[2] + got_d[slot, 2]

    def add_thin(slot, peer):
        thin(0, slot, peer).wait_recv()
        source[...] = source[...] + got_b[slot]

    each_source(add_head)
    invert(node, x, tile, work, lambda: each_source(add_tail))

    @pl.when(inside)
    def _():
        coupled(1, me + 1).wait_recv()

        @pl.when(odd)
        def _():
            coupled(0, me - 1).wait_recv()
            first_link(me - 1).wait_send()

        def serve(role, slot, peer, weights, turned):
            weights[top, :] = dot(turned[top, :], x[...])
            send_d[role, 0] = -dot_nt(weights[top, :], turned[top, :])
            go = inside if role == 0 else has_q

            @pl.when(go)
            def _():
                head(role, slot, peer).start()

            send_d[role, 1] = -dot_nt(weights[top, :], turned[low, :])
            weights[low, :] = dot(turned[low, :], x[...])
            send_d[role, 2] = -dot_nt(weights[low, :], turned[low, :])

            @pl.when(go)
            def _():
                tail(role, slot, peer).start()

        serve(0, slot_p, peer_p, w_p, got_link.at[up])
        serve(1, slot_q, peer_q, w_q, got_link.at[1 - up])

        @pl.when(peer_p < total - 1)
        def _():
            send_m[...] = -dot_nt(w_q[...], got_link[up])
            coupled(1 - up, peer_p).start()

    each_source(add_thin)
    keep_y[inner] = dot(x[...], source[...])
    value[...] = keep_y[inner]

    @pl.when(inside)
    def _():
        send_b[0] = -dot(got_link[up], keep_y[inner])
        thin(0, slot_p, peer_p).start()

        @pl.when(has_q)
        def _():
            send_b[1] = -dot(got_link[1 - up], keep_y[inner])
            thin(1, slot_q, peer_q).start()

        keep_p[inner] = dot_nt(x[...], got_link[up])
        keep_q[inner] = dot_nt(x[...], got_link[1 - up])

        @pl.when(has_q)
        def _():
            copy(value, got_x.at[1], sent_value.at[0], come_x.at[1], peer_q).wait_recv()
            value[...] = value[...] - dot(keep_q[inner], got_x[1])

        copy(value, got_x.at[0], sent_value.at[0], come_x.at[0], peer_p).wait_recv()
        value[...] = value[...] - dot(keep_p[inner], got_x[0])

    def hand_down(act):
        for i, s in reversed(list(enumerate(strides))):
            role = jnp.where(level == i + 1, 0, 1)
            for way, (ok, peer) in enumerate(((me >= s, me - s), (me + s < total, me + s))):

                @pl.when(jnp.logical_and(parents[i], ok))
                def _():
                    act(
                        copy(
                            value, got_x.at[role], sent_value.at[2 * i + way], come_x.at[role], peer
                        )
                    )

        @pl.when(even)
        def _():
            act(copy(value, before, sent_value.at[2 * depth], come_x.at[2], me + 1))

    hand_down(lambda c: c.start())
    out[inner] = value[...]
    for i in reversed(range(inner)):
        out[i] = keep_y[i] - dot(keep_q[i], out[i + 1])

    @pl.when(jnp.logical_and(even, me > 0))
    def _():
        for i in reversed(range(inner)):
            out[i] = out[i] - dot(keep_p[i], got_x[up])

    @pl.when(odd)
    def _():
        copy(value, before, sent_value.at[2 * depth], come_x.at[2], me - 1).wait_recv()
        for i in reversed(range(inner)):
            out[i] = out[i] - dot(keep_p[i], before[...])

    @pl.when(inside)
    def _():
        head(0, slot_p, peer_p).wait_send()
        tail(0, slot_p, peer_p).wait_send()
        thin(0, slot_p, peer_p).wait_send()

        @pl.when(peer_p < total - 1)
        def _():
            coupled(1 - up, peer_p).wait_send()

        @pl.when(has_q)
        def _():
            head(1, slot_q, peer_q).wait_send()
            tail(1, slot_q, peer_q).wait_send()
            thin(1, slot_q, peer_q).wait_send()

    hand_down(lambda c: c.wait_send())

    @pl.when(me > 0)
    def _():
        first_head(me - 1).wait_send()
        first_tail(me - 1).wait_send()
        first_thin(me - 1).wait_send()

    @pl.when(jnp.logical_and(odd, root))
    def _():
        first_link(me - 1).wait_send()


def local(runs, total, diag_blocks, coupling, rhs):
    slabs, order = diag_blocks.shape[1:3]
    half = order // 2
    columns = rhs.shape[3]
    depth = total.bit_length() - 1
    square, thin = (order, order), (order, columns)
    vmem = lambda *shape: pltpu.VMEM(shape, jnp.float32)
    dma = lambda n: pltpu.SemaphoreType.DMA((n,))
    slots = 1 + 2 * depth
    result = pl.pallas_call(
        functools.partial(kernel, runs, total),
        out_shape=jax.ShapeDtypeStruct(rhs.shape[1:], jnp.float32),
        in_specs=[pl.BlockSpec(memory_space=pltpu.VMEM)] * 3,
        out_specs=pl.BlockSpec(memory_space=pltpu.VMEM),
        scratch_shapes=[
            vmem(*square),
            vmem(half, half),
            vmem(2, half, half),
            vmem(3, half, half),
            vmem(*thin),
            vmem(*square),
            vmem(*square),
            vmem(*square),
            vmem(slabs, *square),
            vmem(slabs, *square),
            vmem(slabs, *thin),
            vmem(2, 3, half, half),
            vmem(*square),
            vmem(2, *thin),
            vmem(3, half, half),
            vmem(*thin),
            vmem(slots, 3, half, half),
            vmem(slots, *thin),
            vmem(2, *square),
            vmem(2, *thin),
            vmem(*thin),
            vmem(*thin),
            dma(7),
            dma(4),
            dma(slots),
            dma(2 * slots),
            dma(slots),
            dma(2),
            dma(3),
        ],
        compiler_params=pltpu.CompilerParams(collective_id=0, has_side_effects=True),
        name="chain_solve",
    )(diag_blocks[0], coupling[0], rhs[0])
    return result[None]


def solution(mesh):
    spec = P("seg", "run", None, None)
    runs = mesh.shape["run"]
    total = runs * mesh.shape["seg"]
    return jax.shard_map(
        functools.partial(local, runs, total),
        mesh=mesh,
        in_specs=(spec, spec, spec),
        out_specs=spec,
        check_vma=False,
    )
```

profile of v0, /device:TPU:23, one launch (start us, length us, event | category | flops | bytes accessed | tf_op | source)
XLA Modules:
  0.0 117.4 jit_solution(13026823276894908219)
XLA Ops:
  0.0 115.7 %chain_solve.1 = f32[2,256,128]{2,1,0:T(8,128)} custom-call(f32[2,256,256]{2,1,0:T(8,128)} %bitcast.5, f32[2,256,256]{2,1,0:T(8,128)} %bitcast.6, f32[2,256,128]{2,1,0:T(8,128)} %bitcast.7), custom_call_target="tpu_custom_call" | custom-call | tf_op jit(solution)/shard_map/chain_solve/pallas_call | solution.py:434
  115.7 1.7 %copy.5 = f32[1,2,256,128]{3,2,1,0:T(8,128)} copy(f32[1,2,256,128]{3,2,1,0:T(8,128)} %bitcast.4) | data formatting | bytes 524288
where the time goes:
time: 119 us; the launch traced here: 117 us
  Pallas kernels  116 us (97%)
  local copies, waits for them, and re-layouts  1.67 us (1%)
    pallas_call x1, Pallas kernels, local(): pl.pallas_call(functools.partial(kernel, runs, total), out_shape=jax.Shap...  116 us

commit v1 on v0

--- a/solution.py
+++ b/solution.py
@@ -10,6 +10,7 @@
 MESH = pl.DeviceIdType.MESH
 HIGH = lax.Precision.HIGHEST
 ROWS = 8
+GROUPS = 2
 LANES = 128
 
 
@@ -23,42 +24,97 @@
     )
 
 
+def spread(x, shape):
+    return jnp.broadcast_to(x, shape)
+
+
+def total_of(terms):
+    while len(terms) > 1:
+        pairs = [terms[t] + terms[t + 1] for t in range(0, len(terms) - 1, 2)]
+        terms = pairs + terms[len(pairs) * 2 :]
+    return terms[0]
+
+
+def three_parts(x):
+    high = x.astype(jnp.bfloat16)
+    rest = x - high.astype(jnp.float32)
+    mid = rest.astype(jnp.bfloat16)
+    low = (rest - mid.astype(jnp.float32)).astype(jnp.bfloat16)
+    return [part.astype(jnp.float32) for part in (high, mid, low)]
+
+
+def outer_product(left, right):
+    lefts = list(zip(*[three_parts(x) for x in left]))
+    rights = list(zip(*[three_parts(x) for x in right]))
+    order = ((0, 0), (0, 1), (1, 0), (1, 1), (0, 2), (2, 0))
+    stack = lambda parts, side: jnp.concatenate(
+        [x for pair in order for x in parts[pair[side]]], axis=0
+    ).astype(jnp.bfloat16)
+    return lax.dot_general(
+        stack(lefts, 0),
+        stack(rights, 1),
+        (((0,), (0,)), ((), ())),
+        preferred_element_type=jnp.float32,
+    )
+
+
+def eliminate_panel(panel, first, sub, lane):
+    shape = panel[0].shape
+    groups = len(panel)
+    width = groups * ROWS
+    cols = [
+        [jnp.where(lane >= 0, spread(p[:, first + j : first + j + 1], shape), 0.0) for p in panel]
+        for j in range(width)
+    ]
+    for j in range(width):
+        own, row = divmod(j, ROWS)
+        here = sub == row
+        inverse = 1.0 / spread(cols[j][own][row : row + 1, :], shape)
+        factor = [jnp.where(here, -1.0, c) if i == own else c for i, c in enumerate(cols[j])]
+        scaled = [f * inverse for f in factor]
+        clear = lambda x, i: jnp.where(here, 0.0, x) if i == own else x
+        for m in range(j + 1, width):
+            line = spread(cols[m][own][row : row + 1, :], shape)
+            if m == j + 1:
+                steps = [(f * line) * inverse for f in factor]
+            else:
+                steps = [s * line for s in scaled]
+            cols[m] = [clear(c, i) - steps[i] for i, c in enumerate(cols[m])]
+        at = lane == first + j
+        line = jnp.where(at, 1.0, spread(panel[own][row : row + 1, :], shape))
+        panel = [
+            clear(jnp.where(at, 0.0, p), i) - scaled[i] * line for i, p in enumerate(panel)
+        ]
+    return panel
+
+
 def spd_inverse_tile(rows):
-    count = len(rows)
-    width = rows[0].shape[1]
-    shape = (ROWS, width)
+    shape = rows[0].shape
     sub = lax.broadcasted_iota(jnp.int32, shape, 0)
     lane = lax.broadcasted_iota(jnp.int32, shape, 1)
     rows = list(rows)
-    for k in range(count):
+    width = GROUPS * ROWS
+    for k in range(0, len(rows), GROUPS):
         first = k * ROWS
-        panel = rows[k]
-        cols = [jnp.broadcast_to(panel[:, first + j : first + j + 1], shape) for j in range(ROWS)]
-        for j in range(ROWS):
-            here = sub == j
-            pivot = jnp.broadcast_to(cols[j][j : j + 1, :], shape)
-            inverse = 1.0 / pivot
-            factor = jnp.where(here, -1.0, cols[j])
-            panel = jnp.where(lane == first + j, jnp.where(here, 1.0, 0.0), panel)
-            line = jnp.broadcast_to(panel[j : j + 1, :], shape)
-            panel = jnp.where(here, 0.0, panel) - (factor * line) * inverse
-            for m in range(j + 1, ROWS):
-                line = jnp.broadcast_to(cols[m][j : j + 1, :], shape)
-                cols[m] = jnp.where(here, 0.0, cols[m]) - (factor * line) * inverse
-        lines = [jnp.broadcast_to(panel[j : j + 1, :], shape) for j in range(ROWS)]
-        inside = jnp.logical_and(lane >= first, lane < first + ROWS)
-        for i in range(count):
-            if i == k:
-                continue
-            old = rows[i]
+        inside = jnp.logical_and(lane >= first, lane < first + width)
+        panel = rows[k : k + GROUPS]
+        columns = [
+            jnp.where(lane < first, -p, jnp.where(inside, 0.0, p)) for p in panel
+        ]
+        panel = eliminate_panel(panel, first, sub, lane)
+        near = range(k + GROUPS, min(k + 2 * GROUPS, len(rows)))
+        for i in near:
             terms = [
-                jnp.broadcast_to(old[:, first + j : first + j + 1], shape) * lines[j]
-                for j in range(ROWS)
+                spread(rows[i][:, first + j : first + j + 1], shape)
+                * spread(panel[j // ROWS][j % ROWS : j % ROWS + 1, :], shape)
+                for j in range(width)
             ]
-            while len(terms) > 1:
-                terms = [terms[t] + terms[t + 1] for t in range(0, len(terms), 2)]
-            rows[i] = jnp.where(inside, 0.0, old) - terms[0]
-        rows[k] = panel
+            rows[i] = jnp.where(inside, 0.0, rows[i]) - total_of(terms)
+        update = outer_product(columns, panel)
+        for i in range(len(rows)):
+            if i < k or i >= k + 2 * GROUPS:
+                rows[i] = jnp.where(inside, 0.0, rows[i]) - update[i * ROWS : (i + 1) * ROWS, :]
+        rows[k : k + GROUPS] = panel
     return rows
 
 

time: 119 us -> 99.5 us (0.84)
  Pallas kernels: 116 us -> 96.5 us
    pallas_call x1, Pallas kernels: 116 us -> 96.5 us  [local(): pl.pallas_call(functools.partial(kernel, runs, total), out_shape=jax.Shap...]
where the time goes in v1:
time: 99.5 us; the launch traced here: 98.2 us
  Pallas kernels  96.5 us (97%)
  local copies, waits for them, and re-layouts  1.67 us (2%)
    pallas_call x1, Pallas kernels, local(): pl.pallas_call(functools.partial(kernel, runs, total), out_shape=jax.Shap...  96.5 us

profile of v1, /device:TPU:23, one launch (start us, length us, event | category | flops | bytes accessed | tf_op | source)
XLA Modules:
  0.0 98.2 jit_solution(7998978084216122278)
XLA Ops:
  0.0 96.5 %chain_solve.1 = f32[2,256,128]{2,1,0:T(8,128)} custom-call(f32[2,256,256]{2,1,0:T(8,128)} %bitcast.5, f32[2,256,256]{2,1,0:T(8,128)} %bitcast.6, f32[2,256,128]{2,1,0:T(8,128)} %bitcast.7), custom_call_target="tpu_custom_call" | custom-call | tf_op jit(solution)/shard_map/chain_solve/pallas_call | solution.py:490
  96.5 1.7 %copy.5 = f32[1,2,256,128]{3,2,1,0:T(8,128)} copy(f32[1,2,256,128]{3,2,1,0:T(8,128)} %bitcast.4) | data formatting | bytes 524288

commit v2 on v1

--- a/solution.py
+++ b/solution.py
@@ -11,6 +11,7 @@
 HIGH = lax.Precision.HIGHEST
 ROWS = 8
 GROUPS = 2
+PIECES = 4
 LANES = 128
 
 
@@ -175,13 +176,16 @@
     got_x,
     before,
     value,
+    passing,
     sent,
     sent_first,
     sent_value,
+    sent_pass,
     come_d,
     come_b,
     come_m,
     come_x,
+    come_pass,
 ):
     slabs, order = diag.shape[:2]
     inner = slabs - 1
@@ -204,6 +208,8 @@
     has_q = jnp.logical_and(inside, jnp.logical_and(peer_q >= 0, peer_q < total))
     slot_p = 1 + 2 * level + (1 - up)
     slot_q = 1 + 2 * level + up
+    bends = bend_strides(runs, total)
+    piece = order // PIECES
 
     def copy(source_ref, target_ref, send_sem, recv_sem, peer):
         return pltpu.make_async_remote_copy(
@@ -217,22 +223,27 @@
 
     barrier = pltpu.get_barrier_semaphore()
     met = [lax.rem(me + 1, s) == 0 for s in strides]
-    peers = sum(
-        jnp.where(jnp.logical_and(here, ok), 1, 0)
+    greeted = [
+        (jnp.logical_and(here, ok), peer)
         for s, here in zip(strides, met)
-        for ok in (me >= s, me + s < total)
-    )
-    for s, here in zip(strides, met):
-        for ok, peer in ((me >= s, me - s), (me + s < total, me + s)):
-
-            @pl.when(jnp.logical_and(here, ok))
-            def _():
-                pl.semaphore_signal(
-                    barrier,
-                    inc=1,
-                    device_id=(lax.rem(peer, runs), lax.div(peer, runs)),
-                    device_id_type=MESH,
-                )
+        for ok, peer in ((me >= s, me - s), (me + s < total, me + s))
+    ]
+    for s in bends:
+        greeted.append((lax.rem(me + 1, 4 * s) == 3 * s, me + s - 1))
+        greeted.append((lax.rem(me + 2, 4 * s) == 0, me + 1 - s))
+        greeted.append((lax.rem(me + 2, 4 * s) == 0, me + 1 - 2 * s))
+        greeted.append((lax.rem(me + 1, 4 * s) == 2 * s, me + 2 * s - 1))
+    peers = sum(jnp.where(ok, 1, 0) for ok, _ in greeted)
+    for ok, peer in greeted:
+
+        @pl.when(ok)
+        def _():
+            pl.semaphore_signal(
+                barrier,
+                inc=1,
+                device_id=(lax.rem(peer, runs), lax.div(peer, runs)),
+                device_id_type=MESH,
+            )
 
     def first_head(peer):
         return copy(first_d.at[0], got_d.at[0, 0], sent_first.at[0], come_d.at[0], peer)
@@ -267,6 +278,26 @@
 
     def coupled(side, peer):
         return copy(send_m, got_link.at[side], sent.at[6], come_m.at[side], peer)
+
+    def to_bend(which, part, peer):
+        rows = pl.ds(part * piece, piece)
+        return copy(
+            send_m.at[rows],
+            passing.at[which, rows],
+            sent.at[6],
+            come_pass.at[which * PIECES + part],
+            peer,
+        )
+
+    def from_bend(which, part, peer):
+        rows = pl.ds(part * piece, piece)
+        return copy(
+            passing.at[which, rows],
+            got_link.at[1, rows],
+            sent_pass.at[which * PIECES + part],
+            come_m.at[1],
+            peer,
+        )
 
     def each_source(act):
         @pl.when(inside)
@@ -357,6 +388,23 @@
     each_source(add_head)
     invert(node, x, tile, work, lambda: each_source(add_tail))
 
+    def serve(role, slot, peer, weights, turned):
+        weights[top, :] = dot(turned[top, :], x[...])
+        send_d[role, 0] = -dot_nt(weights[top, :], turned[top, :])
+        go = inside if role == 0 else has_q
+
+        @pl.when(go)
+        def _():
+            head(role, slot, peer).start()
+
+        send_d[role, 1] = -dot_nt(weights[top, :], turned[low, :])
+        weights[low, :] = dot(turned[low, :], x[...])
+        send_d[role, 2] = -dot_nt(weights[low, :], turned[low, :])
+
+        @pl.when(go)
+        def _():
+            tail(role, slot, peer).start()
+
     @pl.when(inside)
     def _():
         coupled(1, me + 1).wait_recv()
@@ -366,30 +414,27 @@
             coupled(0, me - 1).wait_recv()
             first_link(me - 1).wait_send()
 
-        def serve(role, slot, peer, weights, turned):
-            weights[top, :] = dot(turned[top, :], x[...])
-            send_d[role, 0] = -dot_nt(weights[top, :], turned[top, :])
-            go = inside if role == 0 else has_q
-
-            @pl.when(go)
+        serve(0, slot_p, peer_p, w_p, got_link.at[up])
+
+        @pl.when(peer_p < total - 1)
+        def _():
+            send_m[...] = -dot_nt(got_link[1 - up], w_p[...])
+            bent = [lax.rem(me + 1, 4 * s) == 3 * s for s in bends]
+            for i, s in enumerate(bends):
+
+                @pl.when(bent[i])
+                def _():
+                    for part in range(PIECES):
+                        to_bend(i, part, me + s - 1).start()
+
+            straight = sum(jnp.where(b, 1, 0) for b in bent) == 0
+
+            @pl.when(straight)
             def _():
-                head(role, slot, peer).start()
-
-            send_d[role, 1] = -dot_nt(weights[top, :], turned[low, :])
-            weights[low, :] = dot(turned[low, :], x[...])
-            send_d[role, 2] = -dot_nt(weights[low, :], turned[low, :])
-
-            @pl.when(go)
-            def _():
-                tail(role, slot, peer).start()
-
-        serve(0, slot_p, peer_p, w_p, got_link.at[up])
-        serve(1, slot_q, peer_q, w_q, got_link.at[1 - up])
-
-        @pl.when(peer_p < total - 1)
-        def _():
-            send_m[...] = -dot_nt(w_q[...], got_link[up])
-            coupled(1 - up, peer_p).start()
+                coupled(1 - up, peer_p).start()
+
+        keep_p[inner] = dot_nt(x[...], got_link[up])
+        keep_q[inner] = dot_nt(x[...], got_link[1 - up])
 
     each_source(add_thin)
     keep_y[inner] = dot(x[...], source[...])
@@ -399,14 +444,20 @@
     def _():
         send_b[0] = -dot(got_link[up], keep_y[inner])
         thin(0, slot_p, peer_p).start()
+        serve(1, slot_q, peer_q, w_q, got_link.at[1 - up])
 
         @pl.when(has_q)
         def _():
             send_b[1] = -dot(got_link[1 - up], keep_y[inner])
             thin(1, slot_q, peer_q).start()
 
-        keep_p[inner] = dot_nt(x[...], got_link[up])
-        keep_q[inner] = dot_nt(x[...], got_link[1 - up])
+        for i, s in enumerate(bends):
+
+            @pl.when(lax.rem(me + 2, 4 * s) == 0)
+            def _():
+                for part in range(PIECES):
+                    to_bend(i, part, me).wait_recv()
+                    from_bend(i, part, me + 1 - 2 * s).start()
 
         @pl.when(has_q)
         def _():
@@ -466,6 +517,12 @@
             thin(1, slot_q, peer_q).wait_send()
 
     hand_down(lambda c: c.wait_send())
+    for i, s in enumerate(bends):
+
+        @pl.when(lax.rem(me + 2, 4 * s) == 0)
+        def _():
+            for part in range(PIECES):
+                from_bend(i, part, me + 1 - 2 * s).wait_send()
 
     @pl.when(me > 0)
     def _():
@@ -476,6 +533,11 @@
     @pl.when(jnp.logical_and(odd, root))
     def _():
         first_link(me - 1).wait_send()
+
+
+def bend_strides(runs, total):
+    stride = runs // 2
+    return [stride] if stride > 1 and 4 * stride <= total else []
 
 
 def local(runs, total, diag_blocks, coupling, rhs):
@@ -487,6 +549,7 @@
     vmem = lambda *shape: pltpu.VMEM(shape, jnp.float32)
     dma = lambda n: pltpu.SemaphoreType.DMA((n,))
     slots = 1 + 2 * depth
+    bends = len(bend_strides(runs, total))
     result = pl.pallas_call(
         functools.partial(kernel, runs, total),
         out_shape=jax.ShapeDtypeStruct(rhs.shape[1:], jnp.float32),
@@ -515,13 +578,16 @@
             vmem(2, *thin),
             vmem(*thin),
             vmem(*thin),
+            vmem(bends, *square),
             dma(7),
             dma(4),
             dma(slots),
+            dma(bends * PIECES),
             dma(2 * slots),
             dma(slots),
             dma(2),
             dma(3),
+            dma(bends * PIECES),
         ],
         compiler_params=pltpu.CompilerParams(collective_id=0, has_side_effects=True),
         name="chain_solve",

time: 99.5 us -> 94.7 us (0.952)
  Pallas kernels: 96.5 us -> 91.7 us
    pallas_call x1, Pallas kernels: 96.5 us -> 91.7 us  [local(): pl.pallas_call(functools.partial(kernel, runs, total), out_shape=jax.Shap...]
where the time goes in v2:
time: 94.7 us; the launch traced here: 93.4 us
  Pallas kernels  91.7 us (97%)
  local copies, waits for them, and re-layouts  1.67 us (2%)
    pallas_call x1, Pallas kernels, local(): pl.pallas_call(functools.partial(kernel, runs, total), out_shape=jax.Shap...  91.7 us

profile of v2, /device:TPU:23, one launch (start us, length us, event | category | flops | bytes accessed | tf_op | source)
XLA Modules:
  0.0 93.4 jit_solution(12346904452653242939)
XLA Ops:
  0.0 91.7 %chain_solve.1 = f32[2,256,128]{2,1,0:T(8,128)} custom-call(f32[2,256,256]{2,1,0:T(8,128)} %bitcast.5, f32[2,256,256]{2,1,0:T(8,128)} %bitcast.6, f32[2,256,128]{2,1,0:T(8,128)} %bitcast.7), custom_call_target="tpu_custom_call" | custom-call | tf_op jit(solution)/shard_map/chain_solve/pallas_call | solution.py:553
  91.7 1.7 %copy.5 = f32[1,2,256,128]{3,2,1,0:T(8,128)} copy(f32[1,2,256,128]{3,2,1,0:T(8,128)} %bitcast.4) | data formatting | bytes 524288

commit v3 on v2

--- a/solution.py
+++ b/solution.py
@@ -63,30 +63,32 @@
     shape = panel[0].shape
     groups = len(panel)
     width = groups * ROWS
-    cols = [
-        [jnp.where(lane >= 0, spread(p[:, first + j : first + j + 1], shape), 0.0) for p in panel]
-        for j in range(width)
-    ]
+    cols = [[spread(p[:, first + j : first + j + 1], shape) for p in panel] for j in range(width)]
+    for col in cols:
+        col[0] = jnp.where(lane >= 0, col[0], 0.0)
+    inverses = [jnp.zeros(shape, jnp.float32)] * groups
     for j in range(width):
         own, row = divmod(j, ROWS)
         here = sub == row
         inverse = 1.0 / spread(cols[j][own][row : row + 1, :], shape)
-        factor = [jnp.where(here, -1.0, c) if i == own else c for i, c in enumerate(cols[j])]
+        inverses[own] = jnp.where(here, inverse, inverses[own])
+        factor = [jnp.where(here, 0.0, c) if i == own else c for i, c in enumerate(cols[j])]
         scaled = [f * inverse for f in factor]
-        clear = lambda x, i: jnp.where(here, 0.0, x) if i == own else x
         for m in range(j + 1, width):
             line = spread(cols[m][own][row : row + 1, :], shape)
             if m == j + 1:
                 steps = [(f * line) * inverse for f in factor]
             else:
-                steps = [s * line for s in scaled]
-            cols[m] = [clear(c, i) - steps[i] for i, c in enumerate(cols[m])]
+                steps = [f * line for f in scaled]
+            cols[m] = [c - step for c, step in zip(cols[m], steps)]
         at = lane == first + j
         line = jnp.where(at, 1.0, spread(panel[own][row : row + 1, :], shape))
+        unit = jnp.where(here, 1.0, 0.0)
         panel = [
-            clear(jnp.where(at, 0.0, p), i) - scaled[i] * line for i, p in enumerate(panel)
+            jnp.where(at, unit if i == own else 0.0, p) - scaled[i] * line
+            for i, p in enumerate(panel)
         ]
-    return panel
+    return [p * scale for p, scale in zip(panel, inverses)]
 
 
 def spd_inverse_tile(rows):
@@ -154,6 +156,7 @@
     coup,
     rhs,
     out,
+    first_x,
     x,
     tile,
     work,
@@ -167,6 +170,7 @@
     keep_y,
     send_d,
     send_m,
+    send_t,
     send_b,
     first_d,
     first_b,
@@ -194,18 +198,22 @@
     me = lax.axis_index("seg") * runs + lax.axis_index("run")
     depth = total.bit_length() - 1
     strides = [1 << i for i in range(depth)]
-    root = me == total - 1
-    inside = jnp.logical_not(root)
+    last = me == total - 1
+    inside = jnp.logical_not(last)
+    pair = lax.rem(me + 1, total // 2) == 0
+    single = jnp.logical_not(pair)
+    tells_last = me == total - 1 - total // 4
     even = lax.rem(me, 2) == 0
     odd = jnp.logical_not(even)
-    parents = [lax.rem(me + 1, 2 * s) == 0 for s in strides]
+    steps = strides[:-1]
+    parents = [lax.rem(me + 1, 2 * s) == 0 for s in steps]
     level = sum(jnp.where(parent, 1, 0) for parent in parents)
-    span = 1 + sum(jnp.where(parent, s, 0) for s, parent in zip(strides, parents))
+    span = 1 + sum(jnp.where(parent, s, 0) for s, parent in zip(steps, parents))
     next_above = lax.rem(me + span, 4 * span) == 2 * span - 1
     up = jnp.where(next_above, 1, 0)
     peer_p = jnp.where(next_above, me + span, me - span)
     peer_q = jnp.where(next_above, me - span, me + span)
-    has_q = jnp.logical_and(inside, jnp.logical_and(peer_q >= 0, peer_q < total))
+    has_q = jnp.logical_and(peer_q >= 0, peer_q < total)
     slot_p = 1 + 2 * level + (1 - up)
     slot_q = 1 + 2 * level + up
     bends = bend_strides(runs, total)
@@ -279,6 +287,9 @@
     def coupled(side, peer):
         return copy(send_m, got_link.at[side], sent.at[6], come_m.at[side], peer)
 
+    def mirrored():
+        return copy(send_t, got_link.at[0], sent.at[7], come_m.at[0], total - 1)
+
     def to_bend(which, part, peer):
         rows = pl.ds(part * piece, piece)
         return copy(
@@ -304,7 +315,7 @@
         def _():
             act(0, me + 1)
 
-        for i, s in enumerate(strides):
+        for i, s in enumerate(steps):
             for way, (ok, peer) in enumerate(((me >= s, me - s), (me + s < total, me + s))):
 
                 @pl.when(jnp.logical_and(parents[i], ok))
@@ -319,8 +330,8 @@
     for i in range(inner):
         final = i == inner - 1
         f_turned = coup.at[i + 1]
-        invert(node, x, tile, work, lambda: None)
-        w_p[...] = dot(e_turned[...], x[...])
+        invert(node, first_x, tile, work, lambda: None)
+        w_p[...] = dot(e_turned[...], first_x[...])
 
         def put(block, rows, columns):
             term = dot_nt(w_p[rows, :], e_turned[columns, :])
@@ -342,34 +353,40 @@
             def _():
                 first_tail(me - 1).start()
 
-        w_q[...] = dot(f_turned[...], x[...])
+        w_q[...] = dot(f_turned[...], first_x[...])
         node[0] = diag[i + 1, top, top] - dot_nt(w_q[top, :], f_turned[top, :])
         node[1] = diag[i + 1, top, low] - dot_nt(w_q[top, :], f_turned[low, :])
         node[2] = diag[i + 1, low, low] - dot_nt(w_q[low, :], f_turned[low, :])
+
+        def rest(i):
+            f_turned = coup.at[i + 1]
+            keep_y[i] = dot(first_x[...], source[...])
+            term = dot(e_turned[...], keep_y[i])
+            first_b[...] = -term if i == 0 else first_b[...] - term
+            if i == inner - 1:
+
+                @pl.when(me > 0)
+                def _():
+                    first_thin(me - 1).start()
+
+            source[...] = rhs[i + 1] - dot(f_turned[...], keep_y[i])
+            keep_p[i] = dot_nt(first_x[...], e_turned[...])
+            keep_q[i] = dot_nt(first_x[...], f_turned[...])
+
         if final:
 
             @pl.when(odd)
             def _():
                 send_m[...] = -dot_nt(w_q[...], e_turned[...])
                 first_link(me - 1).start()
+                rest(inner - 1)
 
             @pl.when(even)
             def _():
                 got_link[0] = -dot_nt(w_p[...], f_turned[...])
 
-        keep_y[i] = dot(x[...], source[...])
-        term = dot(e_turned[...], keep_y[i])
-        first_b[...] = -term if i == 0 else first_b[...] - term
-        if final:
-
-            @pl.when(me > 0)
-            def _():
-                first_thin(me - 1).start()
-
-        source[...] = rhs[i + 1] - dot(f_turned[...], keep_y[i])
-        keep_p[i] = dot_nt(x[...], e_turned[...])
-        keep_q[i] = dot_nt(x[...], f_turned[...])
-        if not final:
+        else:
+            rest(i)
             e_turned[...] = -dot_nt(w_p[...], f_turned[...])
 
     def add_head(slot, peer):
@@ -388,76 +405,96 @@
     each_source(add_head)
     invert(node, x, tile, work, lambda: each_source(add_tail))
 
-    def serve(role, slot, peer, weights, turned):
+    def serve_head(role, slot, peer, weights, turned):
         weights[top, :] = dot(turned[top, :], x[...])
         send_d[role, 0] = -dot_nt(weights[top, :], turned[top, :])
-        go = inside if role == 0 else has_q
-
-        @pl.when(go)
-        def _():
-            head(role, slot, peer).start()
-
+        head(role, slot, peer).start()
+
+    def serve_tail(role, slot, peer, weights, turned):
         send_d[role, 1] = -dot_nt(weights[top, :], turned[low, :])
         weights[low, :] = dot(turned[low, :], x[...])
         send_d[role, 2] = -dot_nt(weights[low, :], turned[low, :])
-
-        @pl.when(go)
-        def _():
-            tail(role, slot, peer).start()
+        tail(role, slot, peer).start()
 
     @pl.when(inside)
     def _():
         coupled(1, me + 1).wait_recv()
 
-        @pl.when(odd)
-        def _():
-            coupled(0, me - 1).wait_recv()
-            first_link(me - 1).wait_send()
-
-        serve(0, slot_p, peer_p, w_p, got_link.at[up])
-
-        @pl.when(peer_p < total - 1)
-        def _():
-            send_m[...] = -dot_nt(got_link[1 - up], w_p[...])
-            bent = [lax.rem(me + 1, 4 * s) == 3 * s for s in bends]
-            for i, s in enumerate(bends):
-
-                @pl.when(bent[i])
-                def _():
-                    for part in range(PIECES):
-                        to_bend(i, part, me + s - 1).start()
-
-            straight = sum(jnp.where(b, 1, 0) for b in bent) == 0
-
-            @pl.when(straight)
+    @pl.when(odd)
+    def _():
+        coupled(0, me - 1).wait_recv()
+        first_link(me - 1).wait_send()
+
+    to_p = (0, slot_p, peer_p, w_p, got_link.at[up])
+    to_q = (1, slot_q, peer_q, w_q, got_link.at[1 - up])
+    serve_head(*to_p)
+
+    @pl.when(tells_last)
+    def _():
+        serve_head(*to_q)
+
+    serve_tail(*to_p)
+
+    @pl.when(tells_last)
+    def _():
+        serve_tail(*to_q)
+
+    @pl.when(single)
+    def _():
+        send_m[...] = -dot_nt(got_link[1 - up], w_p[...])
+        bent = [lax.rem(me + 1, 4 * s) == 3 * s for s in bends]
+        for i, s in enumerate(bends):
+
+            @pl.when(bent[i])
             def _():
-                coupled(1 - up, peer_p).start()
+                for part in range(PIECES):
+                    to_bend(i, part, me + s - 1).start()
+
+        straight = sum(jnp.where(b, 1, 0) for b in bent) == 0
+
+        @pl.when(straight)
+        def _():
+            coupled(1 - up, peer_p).start()
+
+        @pl.when(tells_last)
+        def _():
+            send_t[...] = -dot_nt(w_p[...], got_link[1 - up])
+            mirrored().start()
 
         keep_p[inner] = dot_nt(x[...], got_link[up])
         keep_q[inner] = dot_nt(x[...], got_link[1 - up])
 
+    @pl.when(even)
+    def _():
+        rest(inner - 1)
+
     each_source(add_thin)
     keep_y[inner] = dot(x[...], source[...])
-    value[...] = keep_y[inner]
-
-    @pl.when(inside)
-    def _():
-        send_b[0] = -dot(got_link[up], keep_y[inner])
-        thin(0, slot_p, peer_p).start()
-        serve(1, slot_q, peer_q, w_q, got_link.at[1 - up])
-
-        @pl.when(has_q)
-        def _():
-            send_b[1] = -dot(got_link[1 - up], keep_y[inner])
-            thin(1, slot_q, peer_q).start()
-
-        for i, s in enumerate(bends):
-
-            @pl.when(lax.rem(me + 2, 4 * s) == 0)
-            def _():
-                for part in range(PIECES):
-                    to_bend(i, part, me).wait_recv()
-                    from_bend(i, part, me + 1 - 2 * s).start()
+    send_b[0] = -dot(got_link[up], keep_y[inner])
+    thin(0, slot_p, peer_p).start()
+
+    @pl.when(has_q)
+    def _():
+
+        @pl.when(jnp.logical_not(tells_last))
+        def _():
+            serve_head(*to_q)
+            serve_tail(*to_q)
+
+        send_b[1] = -dot(got_link[1 - up], keep_y[inner])
+        thin(1, slot_q, peer_q).start()
+
+    for i, s in enumerate(bends):
+
+        @pl.when(lax.rem(me + 2, 4 * s) == 0)
+        def _():
+            for part in range(PIECES):
+                to_bend(i, part, me).wait_recv()
+                from_bend(i, part, me + 1 - 2 * s).start()
+
+    @pl.when(single)
+    def _():
+        value[...] = keep_y[inner]
 
         @pl.when(has_q)
         def _():
@@ -467,9 +504,17 @@
         copy(value, got_x.at[0], sent_value.at[0], come_x.at[0], peer_p).wait_recv()
         value[...] = value[...] - dot(keep_p[inner], got_x[0])
 
+    @pl.when(pair)
+    def _():
+        slot = 1 + 2 * level + up
+        add_head(slot, peer_p)
+        invert(node, x, tile, work, lambda: add_tail(slot, peer_p))
+        add_thin(slot, peer_p)
+        value[...] = dot(x[...], source[...])
+
     def hand_down(act):
-        for i, s in reversed(list(enumerate(strides))):
-            role = jnp.where(level == i + 1, 0, 1)
+        for i, s in reversed(list(enumerate(steps))):
+            role = jnp.where(jnp.logical_and(level == i + 1, inside), 0, 1)
             for way, (ok, peer) in enumerate(((me >= s, me - s), (me + s < total, me + s))):
 
                 @pl.when(jnp.logical_and(parents[i], ok))
@@ -500,21 +545,23 @@
         for i in reversed(range(inner)):
             out[i] = out[i] - dot(keep_p[i], before[...])
 
-    @pl.when(inside)
-    def _():
-        head(0, slot_p, peer_p).wait_send()
-        tail(0, slot_p, peer_p).wait_send()
-        thin(0, slot_p, peer_p).wait_send()
-
-        @pl.when(peer_p < total - 1)
-        def _():
-            coupled(1 - up, peer_p).wait_send()
-
-        @pl.when(has_q)
-        def _():
-            head(1, slot_q, peer_q).wait_send()
-            tail(1, slot_q, peer_q).wait_send()
-            thin(1, slot_q, peer_q).wait_send()
+    head(0, slot_p, peer_p).wait_send()
+    tail(0, slot_p, peer_p).wait_send()
+    thin(0, slot_p, peer_p).wait_send()
+
+    @pl.when(single)
+    def _():
+        coupled(1 - up, peer_p).wait_send()
+
+    @pl.when(tells_last)
+    def _():
+        mirrored().wait_send()
+
+    @pl.when(has_q)
+    def _():
+        head(1, slot_q, peer_q).wait_send()
+        tail(1, slot_q, peer_q).wait_send()
+        thin(1, slot_q, peer_q).wait_send()
 
     hand_down(lambda c: c.wait_send())
     for i, s in enumerate(bends):
@@ -529,10 +576,6 @@
         first_head(me - 1).wait_send()
         first_tail(me - 1).wait_send()
         first_thin(me - 1).wait_send()
-
-    @pl.when(jnp.logical_and(odd, root))
-    def _():
-        first_link(me - 1).wait_send()
 
 
 def bend_strides(runs, total):
@@ -557,6 +600,7 @@
         out_specs=pl.BlockSpec(memory_space=pltpu.VMEM),
         scratch_shapes=[
             vmem(*square),
+            vmem(*square),
             vmem(half, half),
             vmem(2, half, half),
             vmem(3, half, half),
@@ -569,6 +613,7 @@
             vmem(slabs, *thin),
             vmem(2, 3, half, half),
             vmem(*square),
+            vmem(*square),
             vmem(2, *thin),
             vmem(3, half, half),
             vmem(*thin),
@@ -579,7 +624,7 @@
             vmem(*thin),
             vmem(*thin),
             vmem(bends, *square),
-            dma(7),
+            dma(8),
             dma(4),
             dma(slots),
             dma(bends * PIECES),

time: 94.7 us -> 88.5 us (0.935)
  Pallas kernels: 91.7 us -> 85.6 us
    pallas_call x1, Pallas kernels: 91.7 us -> 85.6 us  [local(): pl.pallas_call(functools.partial(kernel, runs, total), out_shape=jax.Shap...]
where the time goes in v3:
time: 88.5 us; the launch traced here: 87.3 us
  Pallas kernels  85.6 us (97%)
  local copies, waits for them, and re-layouts  1.67 us (2%)
    pallas_call x1, Pallas kernels, local(): pl.pallas_call(functools.partial(kernel, runs, total), out_shape=jax.Shap...  85.6 us

profile of v3, /device:TPU:23, one launch (start us, length us, event | category | flops | bytes accessed | tf_op | source)
XLA Modules:
  0.0 87.3 jit_solution(7373936942453024829)
XLA Ops:
  0.0 85.6 %chain_solve.1 = f32[2,256,128]{2,1,0:T(8,128)} custom-call(f32[2,256,256]{2,1,0:T(8,128)} %bitcast.5, f32[2,256,256]{2,1,0:T(8,128)} %bitcast.6, f32[2,256,128]{2,1,0:T(8,128)} %bitcast.7), custom_call_target="tpu_custom_call" | custom-call | tf_op jit(solution)/shard_map/chain_solve/pallas_call | solution.py:596
  85.6 1.7 %copy.5 = f32[1,2,256,128]{3,2,1,0:T(8,128)} copy(f32[1,2,256,128]{3,2,1,0:T(8,128)} %bitcast.4) | data formatting | bytes 524288

commit v4 on v3

--- a/solution.py
+++ b/solution.py
@@ -12,6 +12,7 @@
 ROWS = 8
 GROUPS = 2
 PIECES = 4
+PAUSE = 12
 LANES = 128
 
 
@@ -181,15 +182,19 @@
     before,
     value,
     passing,
+    far_k,
+    far_y,
     sent,
     sent_first,
     sent_value,
     sent_pass,
+    sent_far,
     come_d,
     come_b,
     come_m,
     come_x,
     come_pass,
+    come_far,
 ):
     slabs, order = diag.shape[:2]
     inner = slabs - 1
@@ -203,6 +208,9 @@
     pair = lax.rem(me + 1, total // 2) == 0
     single = jnp.logical_not(pair)
     tells_last = me == total - 1 - total // 4
+    reach = total // 8
+    gives = lax.rem(me + 1, 4 * reach) == 2 * reach
+    takes = lax.rem(me + 1, 2 * reach) == reach
     even = lax.rem(me, 2) == 0
     odd = jnp.logical_not(even)
     steps = strides[:-1]
@@ -216,6 +224,8 @@
     has_q = jnp.logical_and(peer_q >= 0, peer_q < total)
     slot_p = 1 + 2 * level + (1 - up)
     slot_q = 1 + 2 * level + up
+    far = jnp.where(next_above, me + 3 * reach, me - 3 * reach)
+    has_far = jnp.logical_and(far >= 0, far < total)
     bends = bend_strides(runs, total)
     piece = order // PIECES
 
@@ -236,6 +246,10 @@
         for s, here in zip(strides, met)
         for ok, peer in ((me >= s, me - s), (me + s < total, me + s))
     ]
+    for peer in (me - 3 * reach, me + 3 * reach):
+        ok = jnp.logical_and(peer >= 0, peer < total)
+        greeted.append((jnp.logical_and(lax.rem(me + 1, 4 * reach) == 0, ok), peer))
+    greeted.append((jnp.logical_and(takes, has_far), far))
     for s in bends:
         greeted.append((lax.rem(me + 1, 4 * s) == 3 * s, me + s - 1))
         greeted.append((lax.rem(me + 2, 4 * s) == 0, me + 1 - s))
@@ -309,6 +323,17 @@
             come_m.at[1],
             peer,
         )
+
+    def each_gift(act):
+        for way, peer in enumerate((me - reach, me + reach)):
+            for k, (source_ref, target_ref) in enumerate(
+                (
+                    (keep_p.at[inner], far_k.at[up]),
+                    (keep_q.at[inner], far_k.at[1 - up]),
+                    (keep_y.at[inner], far_y),
+                )
+            ):
+                act(copy(source_ref, target_ref, sent_far.at[3 * way + k], come_far.at[k], peer))
 
     def each_source(act):
         @pl.when(inside)
@@ -478,6 +503,10 @@
 
         @pl.when(jnp.logical_not(tells_last))
         def _():
+            @pl.loop(0, jnp.where(level == 1, PAUSE, 0))
+            def _(_):
+                tile[...] = tile[...].T
+
             serve_head(*to_q)
             serve_tail(*to_q)
 
@@ -492,17 +521,33 @@
                 to_bend(i, part, me).wait_recv()
                 from_bend(i, part, me + 1 - 2 * s).start()
 
+    @pl.when(gives)
+    def _():
+        each_gift(lambda c: c.start())
+
     @pl.when(single)
     def _():
         value[...] = keep_y[inner]
 
+    @pl.when(takes)
+    def _():
+        for k, target_ref in enumerate((far_k.at[up], far_k.at[1 - up], far_y)):
+            copy(target_ref, target_ref, sent_far.at[k], come_far.at[k], peer_p).wait_recv()
+        value[...] = value[...] - dot(keep_p[inner], far_y[...])
+        keep_q[inner] = keep_q[inner] - dot(keep_p[inner], far_k[1 - up])
+        keep_p[inner] = -dot(keep_p[inner], far_k[up])
+
+    @pl.when(single)
+    def _():
         @pl.when(has_q)
         def _():
             copy(value, got_x.at[1], sent_value.at[0], come_x.at[1], peer_q).wait_recv()
             value[...] = value[...] - dot(keep_q[inner], got_x[1])
 
-        copy(value, got_x.at[0], sent_value.at[0], come_x.at[0], peer_p).wait_recv()
-        value[...] = value[...] - dot(keep_p[inner], got_x[0])
+        @pl.when(jnp.logical_or(jnp.logical_not(takes), has_far))
+        def _():
+            copy(value, got_x.at[0], sent_value.at[0], come_x.at[0], peer_p).wait_recv()
+            value[...] = value[...] - dot(keep_p[inner], got_x[0])
 
     @pl.when(pair)
     def _():
@@ -513,11 +558,14 @@
         value[...] = dot(x[...], source[...])
 
     def hand_down(act):
-        for i, s in reversed(list(enumerate(steps))):
+        def near(i, s):
             role = jnp.where(jnp.logical_and(level == i + 1, inside), 0, 1)
+            tells = parents[i]
+            if s == reach:
+                tells = jnp.logical_and(tells, jnp.logical_not(gives))
             for way, (ok, peer) in enumerate(((me >= s, me - s), (me + s < total, me + s))):
 
-                @pl.when(jnp.logical_and(parents[i], ok))
+                @pl.when(jnp.logical_and(tells, ok))
                 def _():
                     act(
                         copy(
@@ -525,6 +573,19 @@
                         )
                     )
 
+        order_of = list(enumerate(steps))
+        near(*order_of[-2])
+        for way, peer in enumerate((me - 3 * reach, me + 3 * reach)):
+            ok = jnp.logical_and(peer >= 0, peer < total)
+
+            @pl.when(jnp.logical_and(lax.rem(me + 1, 4 * reach) == 0, ok))
+            def _():
+                act(copy(value, got_x.at[0], sent_far.at[6 + way], come_x.at[0], peer))
+
+        near(*order_of[-1])
+        for i, s in reversed(order_of[:-2]):
+            near(i, s)
+
         @pl.when(even)
         def _():
             act(copy(value, before, sent_value.at[2 * depth], come_x.at[2], me + 1))
@@ -556,6 +617,10 @@
     @pl.when(tells_last)
     def _():
         mirrored().wait_send()
+
+    @pl.when(gives)
+    def _():
+        each_gift(lambda c: c.wait_send())
 
     @pl.when(has_q)
     def _():
@@ -624,15 +689,19 @@
             vmem(*thin),
             vmem(*thin),
             vmem(bends, *square),
+            vmem(2, *square),
+            vmem(*thin),
             dma(8),
             dma(4),
             dma(slots),
             dma(bends * PIECES),
+            dma(8),
             dma(2 * slots),
             dma(slots),
             dma(2),
             dma(3),
             dma(bends * PIECES),
+            dma(3),
         ],
         compiler_params=pltpu.CompilerParams(collective_id=0, has_side_effects=True),
         name="chain_solve",

time: 88.5 us -> 86.4 us (0.976); the launches traced: 87.3 us -> 86.3 us
  Pallas kernels: 85.6 us -> 84.6 us
    pallas_call x1, Pallas kernels: 85.6 us -> 84.6 us  [local(): pl.pallas_call(functools.partial(kernel, runs, total), out_shape=jax.Shap...]
where the time goes in v4:
time: 86.4 us; the launch traced here: 86.3 us
  Pallas kernels  84.6 us (98%)
  local copies, waits for them, and re-layouts  1.67 us (2%)
    pallas_call x1, Pallas kernels, local(): pl.pallas_call(functools.partial(kernel, runs, total), out_shape=jax.Shap...  84.6 us

profile of v4, /device:TPU:23, one launch (start us, length us, event | category | flops | bytes accessed | tf_op | source)
XLA Modules:
  0.0 86.3 jit_solution(16467410738635756734)
XLA Ops:
  0.0 84.6 %chain_solve.1 = f32[2,256,128]{2,1,0:T(8,128)} custom-call(f32[2,256,256]{2,1,0:T(8,128)} %bitcast.5, f32[2,256,256]{2,1,0:T(8,128)} %bitcast.6, f32[2,256,128]{2,1,0:T(8,128)} %bitcast.7), custom_call_target="tpu_custom_call" | custom-call | tf_op jit(solution)/shard_map/chain_solve/pallas_call | solution.py:661
  84.6 1.7 %copy.5 = f32[1,2,256,128]{3,2,1,0:T(8,128)} copy(f32[1,2,256,128]{3,2,1,0:T(8,128)} %bitcast.4) | data formatting | bytes 524288

commit v5 on v4

--- a/solution.py
+++ b/solution.py
@@ -12,7 +12,7 @@
 ROWS = 8
 GROUPS = 2
 PIECES = 4
-PAUSE = 12
+PAUSE = 8
 LANES = 128
 
 
@@ -65,8 +65,7 @@
     groups = len(panel)
     width = groups * ROWS
     cols = [[spread(p[:, first + j : first + j + 1], shape) for p in panel] for j in range(width)]
-    for col in cols:
-        col[0] = jnp.where(lane >= 0, col[0], 0.0)
+    cols[0] = [jnp.where(lane >= 0, c, 0.0) for c in cols[0]]
     inverses = [jnp.zeros(shape, jnp.float32)] * groups
     for j in range(width):
         own, row = divmod(j, ROWS)
@@ -76,7 +75,8 @@
         factor = [jnp.where(here, 0.0, c) if i == own else c for i, c in enumerate(cols[j])]
         scaled = [f * inverse for f in factor]
         for m in range(j + 1, width):
-            line = spread(cols[m][own][row : row + 1, :], shape)
+            at_m, row_m = divmod(m, ROWS)
+            line = spread(cols[j][at_m][row_m : row_m + 1, :], shape)
             if m == j + 1:
                 steps = [(f * line) * inverse for f in factor]
             else:
@@ -537,16 +537,31 @@
         keep_q[inner] = keep_q[inner] - dot(keep_p[inner], far_k[1 - up])
         keep_p[inner] = -dot(keep_p[inner], far_k[up])
 
+    passes = jnp.logical_and(level == 1, me >= 2)
+
+    def passed(side):
+        return copy(got_x.at[side], got_x.at[1], sent_pass.at[len(bends) * PIECES], come_x.at[1], me - 1)
+
     @pl.when(single)
     def _():
         @pl.when(has_q)
         def _():
             copy(value, got_x.at[1], sent_value.at[0], come_x.at[1], peer_q).wait_recv()
+
+            @pl.when(jnp.logical_and(passes, up == 1))
+            def _():
+                passed(1).start()
+
             value[...] = value[...] - dot(keep_q[inner], got_x[1])
 
         @pl.when(jnp.logical_or(jnp.logical_not(takes), has_far))
         def _():
             copy(value, got_x.at[0], sent_value.at[0], come_x.at[0], peer_p).wait_recv()
+
+            @pl.when(jnp.logical_and(passes, up == 0))
+            def _():
+                passed(0).start()
+
             value[...] = value[...] - dot(keep_p[inner], got_x[0])
 
     @pl.when(pair)
@@ -564,6 +579,8 @@
             if s == reach:
                 tells = jnp.logical_and(tells, jnp.logical_not(gives))
             for way, (ok, peer) in enumerate(((me >= s, me - s), (me + s < total, me + s))):
+                if s == 1 and way == 1:
+                    ok = jnp.logical_and(ok, level == 1)
 
                 @pl.when(jnp.logical_and(tells, ok))
                 def _():
@@ -621,6 +638,10 @@
     @pl.when(gives)
     def _():
         each_gift(lambda c: c.wait_send())
+
+    @pl.when(passes)
+    def _():
+        passed(0).wait_send()
 
     @pl.when(has_q)
     def _():
@@ -694,7 +715,7 @@
             dma(8),
             dma(4),
             dma(slots),
-            dma(bends * PIECES),
+            dma(bends * PIECES + 1),
             dma(8),
             dma(2 * slots),
             dma(slots),

time: 86.4 us -> 86.4 us (level)
  no operation moved by 1% of the time
where the time goes in v5:
time: 86.4 us; the launch traced here: 85.4 us
  Pallas kernels  83.8 us (97%)
  local copies, waits for them, and re-layouts  1.67 us (2%)
    pallas_call x1, Pallas kernels, local(): pl.pallas_call(functools.partial(kernel, runs, total), out_shape=jax.Shap...  83.8 us

profile of v5, /device:TPU:23, one launch (start us, length us, event | category | flops | bytes accessed | tf_op | source)
XLA Modules:
  0.0 85.4 jit_solution(16988939038187014524)
XLA Ops:
  0.0 83.8 %chain_solve.1 = f32[2,256,128]{2,1,0:T(8,128)} custom-call(f32[2,256,256]{2,1,0:T(8,128)} %bitcast.5, f32[2,256,256]{2,1,0:T(8,128)} %bitcast.6, f32[2,256,128]{2,1,0:T(8,128)} %bitcast.7), custom_call_target="tpu_custom_call" | custom-call | tf_op jit(solution)/shard_map/chain_solve/pallas_call | solution.py:682
  83.8 1.7 %copy.5 = f32[1,2,256,128]{3,2,1,0:T(8,128)} copy(f32[1,2,256,128]{3,2,1,0:T(8,128)} %bitcast.4) | data formatting | bytes 524288

commit v6 on v5

--- a/solution.py
+++ b/solution.py
@@ -12,7 +12,8 @@
 ROWS = 8
 GROUPS = 2
 PIECES = 4
-PAUSE = 8
+PAUSE = 11
+PAUSE_THIN = 20
 LANES = 128
 
 
@@ -496,6 +497,12 @@
     each_source(add_thin)
     keep_y[inner] = dot(x[...], source[...])
     send_b[0] = -dot(got_link[up], keep_y[inner])
+    crosses = sum(jnp.where(lax.rem(me + 1, 4 * s) == 3 * s, 1, 0) for s in bends)
+
+    @pl.loop(0, crosses * PAUSE_THIN)
+    def _(_):
+        tile[...] = tile[...].T
+
     thin(0, slot_p, peer_p).start()
 
     @pl.when(has_q)

time: 86.4 us -> 84.9 us (0.983)
  Pallas kernels: 83.8 us -> 82.3 us
    pallas_call x1, Pallas kernels: 83.8 us -> 82.3 us  [local(): pl.pallas_call(functools.partial(kernel, runs, total), out_shape=jax.Shap...]
where the time goes in v6:
time: 84.9 us; the launch traced here: 84 us
  Pallas kernels  82.3 us (97%)
  local copies, waits for them, and re-layouts  1.67 us (2%)
    pallas_call x1, Pallas kernels, local(): pl.pallas_call(functools.partial(kernel, runs, total), out_shape=jax.Shap...  82.3 us

profile of v6, /device:TPU:23, one launch (start us, length us, event | category | flops | bytes accessed | tf_op | source)
XLA Modules:
  0.0 84.0 jit_solution(5815048700071714749)
XLA Ops:
  0.0 82.3 %chain_solve.1 = f32[2,256,128]{2,1,0:T(8,128)} custom-call(f32[2,256,256]{2,1,0:T(8,128)} %bitcast.5, f32[2,256,256]{2,1,0:T(8,128)} %bitcast.6, f32[2,256,128]{2,1,0:T(8,128)} %bitcast.7), custom_call_target="tpu_custom_call" | custom-call | tf_op jit(solution)/shard_map/chain_solve/pallas_call | solution.py:689
  82.3 1.7 %copy.5 = f32[1,2,256,128]{3,2,1,0:T(8,128)} copy(f32[1,2,256,128]{3,2,1,0:T(8,128)} %bitcast.4) | data formatting | bytes 524288
